TPU v7x, 512 devices: a whole 4x4x16 slice. The times are simulated.
512 devices in a mesh: shard: 128 (over z, x, core), tensor: 4 (over y).
Axes of the slice: x: 4, y: 4, z: 16, core: 2. Of those that a mesh axis runs over, the one named last changes fastest.
Arguments:
- grads: bfloat16 [128, 4, 1536, 1024], P('shard', None, None, 'tensor'), may hold values from -240 to 240
- master: float32 [1536, 1024], P('shard', 'tensor'), may hold values from -3 to 3
- moment1: float32 [1536, 1024], P('shard', 'tensor'), may hold values from -3 to 3
- moment2: float32 [1536, 1024], P('shard', 'tensor'), may hold values from 0.25 to 1
- ema: float32 [1536, 1024], P('shard', 'tensor'), may hold values from -3 to 3
Outputs:
- new_master: float32 [1536, 1024], P('shard', 'tensor')
- new_moment1: float32 [1536, 1024], P('shard', 'tensor')
- new_moment2: float32 [1536, 1024], P('shard', 'tensor')
- new_ema: float32 [1536, 1024], P('shard', 'tensor')
- weights: bfloat16 [1536, 1024], P(None, 'tensor')
All inputs are finite; a program needn't handle non-finite values.
Results may differ from a plain program's by a relative error of at most 0.0004.
Values may be sent and summed in bfloat16 or wider, within the bound.
No kernel may reach another device: no remote copies, remote signals or barrier semaphores. Data moves between devices by JAX's collectives and lax.ppermute only.
A program may use at most 64 MiB of HBM per device.

v0:
```python
import jax
import jax.numpy as jnp
from jax import lax
from jax.sharding import PartitionSpec as P

STEP = 10
beta_one = 0.9
beta_two = 0.95
learn_rate = 0.02
decay_weight = 0.1
ema_keep = 0.99


def shards(grads, master, moment1, moment2, ema):
    local = grads[0]
    elements = local.shape[1] * local.shape[2] * lax.axis_size("tensor")
    summed = jnp.sum(local.astype(jnp.float32), axis=0)
    grad_part = lax.psum_scatter(summed, "shard", scatter_dimension=0, tiled=True)
    sq = lax.psum(jnp.sum(grad_part * grad_part), ("shard", "tensor"))
    scale = jnp.minimum(1.0, 1.0 / jnp.sqrt(sq / elements + 1e-06))
    clipped = scale * grad_part
    new_moment1 = beta_one * moment1 + (1.0 - beta_one) * clipped
    new_moment2 = beta_two * moment2 + (1.0 - beta_two) * clipped * clipped
    first_hat = new_moment1 / (1.0 - beta_one**STEP)
    second_hat = new_moment2 / (1.0 - beta_two**STEP)
    new_master = master - learn_rate * (
        first_hat / (jnp.sqrt(second_hat) + 1e-08) + decay_weight * master
    )
    new_ema = ema_keep * ema + (1.0 - ema_keep) * new_master
    weights = lax.all_gather(new_master.astype(jnp.bfloat16), "shard", axis=0, tiled=True)
    return (new_master, new_moment1, new_moment2, new_ema, weights)


def solution(mesh):
    return jax.shard_map(
        shards,
        mesh=mesh,
        in_specs=(
            P("shard", None, None, "tensor"),
            P("shard", "tensor"),
            P("shard", "tensor"),
            P("shard", "tensor"),
            P("shard", "tensor"),
        ),
        out_specs=(
            P("shard", "tensor"),
            P("shard", "tensor"),
            P("shard", "tensor"),
            P("shard", "tensor"),
            P(None, "tensor"),
        ),
        check_vma=False,
    )
```

profile of v0, /device:TPU:1, one launch (start us, length us, event | category | flops | bytes accessed | tf_op | source)
XLA Modules:
  0.0 570.4 jit_solution(2033311778829565577)
XLA Ops:
  0.6 2.5 convert_reduce_fusion
  3.1 0.0 copy-start.2
  3.1 0.0 copy-start.3
  3.1 0.0 copy-start.4
  3.2 262.6 %fusion = f32[16,256]{1,0:T(8,128)S(1)} fusion(f32[1536,256]{1,0:T(8,128)S(1)} %convert_reduce_fusion), kind=kCustom, calls=%all-reduce-scatter | all-reduce-scatter fusion | flops 524289 | bytes 1591296
  265.8 0.0 copy-start.1
  265.8 3.0 collective-permute-start
  268.9 2.6 collective-permute-start.31
  271.5 1.3 collective-permute-start.1
  272.8 1.3 collective-permute-start.10
  274.1 2.4 collective-permute-start.11
  276.5 0.0 collective-permute-done.31
  276.5 7.0 %collective-permute-start.12 = (f32[16,256]{1,0:T(8,128)S(1)}, f32[16,256]{1,0:T(8,128)S(1)}, u32[]{:S(2)}, u32[]{:S(2)}) collective-permute-start(f32[16,256]{1,0:T(8,128)S(1)} %fusion), channel_id=1, source_target_pairs={{0,52},{4,56},{8,60},{12,64},{16,68},{20,72},{24,76},{28,80},{32,8... | collective-permute-start | bytes 49160
  283.6 5.3 collective-permute-start.13
  288.9 0.0 collective-permute-done.1
  288.9 8.9 %collective-permute-start.14 = (f32[16,256]{1,0:T(8,128)S(1)}, f32[16,256]{1,0:T(8,128)S(1)}, u32[]{:S(2)}, u32[]{:S(2)}) collective-permute-start(f32[16,256]{1,0:T(8,128)S(1)} %fusion), channel_id=1, source_target_pairs={{0,60},{4,64},{8,68},{12,72},{16,76},{20,80},{24,84},{28,88},{32,9... | collective-permute-start | bytes 49160
  297.8 1.3 collective-permute-start.15
  299.1 6.5 %collective-permute-start.16 = (f32[16,256]{1,0:T(8,128)S(1)}, f32[16,256]{1,0:T(8,128)S(1)}, u32[]{:S(2)}, u32[]{:S(2)}) collective-permute-start(f32[16,256]{1,0:T(8,128)S(1)} %fusion), channel_id=1, source_target_pairs={{0,68},{4,72},{8,76},{12,80},{16,84},{20,88},{24,92},{28,96},{32,1... | collective-permute-start | bytes 49160
  305.6 2.8 collective-permute-start.17
  308.4 4.0 collective-permute-start.18
  312.4 2.9 collective-permute-start.19
  315.3 3.0 collective-permute-start.2
  318.3 1.4 collective-permute-start.20
  319.7 2.7 collective-permute-start.21
  322.4 1.3 collective-permute-start.22
  323.7 1.3 collective-permute-start.23
  325.0 1.8 collective-permute-start.24
  326.9 1.6 collective-permute-start.25
  328.5 3.2 collective-permute-start.26
  331.8 2.8 collective-permute-start.27
  334.7 1.9 collective-permute-start.28
  336.6 1.6 collective-permute-start.29
  338.2 2.6 collective-permute-start.3
  340.9 1.8 collective-permute-start.30
  342.7 4.5 collective-permute-start.4
  347.2 1.3 collective-permute-start.5
  348.5 2.2 collective-permute-start.6
  350.8 3.0 collective-permute-start.7
  353.8 3.7 collective-permute-start.8
  357.5 1.3 collective-permute-start.9
  358.8 1.3 dynamic-slice.4
  360.7 3.7 concatenate
  364.4 0.6 multiply_reduce_fusion
  365.0 102.4 %psum.7 = f32[]{:T(128)} all-reduce(f32[]{:T(128)} %multiply_reduce_fusion), channel_id=1, replica_groups=mesh['shard'=128,'tensor'=4] {'shard','tensor'}, use_global_device_ids=true, to_apply=%region_3.0 | all-reduce | flops 1 | bytes 8 | tf_op jit(solution)/shard_map/psum | solution.py:19
  468.1 0.6 convert_bitcast_fusion
  468.7 100.0 %all-gather = bf16[128,12,256]{2,1,0:T(8,128)(2,1)S(1)} all-gather(bf16[1,12,256]{2,1,0:T(8,128)(2,1)S(1)} %get-tuple-element.5), channel_id=1, replica_groups=mesh['shard'=128,'tensor'=4] {'shard'}, dimensions={0}, use_global_device_ids=true | all-gather | bytes 792576 | tf_op jit(solution)/shard_map/all_gather | solution.py:30
  568.7 1.1 reshape.12
  569.7 0.6 multiply_add_fusion
  (37 shorter events, 0.1 us)
Async XLA Ops:
  3.1 465.0 %copy-start.2 = (f32[12,256]{1,0:T(8,128)S(1)}, f32[12,256]{1,0:T(8,128)}, u32[]{:S(2)}) copy-start(f32[12,256]{1,0:T(8,128)} %param.6) | copy-start | bytes 36868
  3.1 464.9 %copy-start.3 = (f32[12,256]{1,0:T(8,128)S(1)}, f32[12,256]{1,0:T(8,128)}, u32[]{:S(2)}) copy-start(f32[12,256]{1,0:T(8,128)} %param.7) | copy-start | bytes 36868
  3.1 464.9 %copy-start.4 = (f32[12,256]{1,0:T(8,128)S(1)}, f32[12,256]{1,0:T(8,128)}, u32[]{:S(2)}) copy-start(f32[12,256]{1,0:T(8,128)} %param.8) | copy-start | bytes 36868
  265.8 303.9 %copy-start.1 = (f32[12,256]{1,0:T(8,128)S(1)}, f32[12,256]{1,0:T(8,128)}, u32[]{:S(2)}) copy-start(f32[12,256]{1,0:T(8,128)} %param.9) | copy-start | bytes 36868
  265.8 17.7 %collective-permute-start = (f32[16,256]{1,0:T(8,128)S(1)}, f32[16,256]{1,0:T(8,128)S(1)}, u32[]{:S(2)}, u32[]{:S(2)}) collective-permute-start(f32[16,256]{1,0:T(8,128)S(1)} %fusion), channel_id=1, source_target_pairs={{0,4},{4,8},{8,12},{12,16},{16,20},{20,24},{24,28},{28,32},{32,36}... | collective-permute-start | bytes 49160
  268.9 7.7 %collective-permute-start.31 = (f32[12,256]{1,0:T(8,128)S(1)}, f32[12,256]{1,0:T(8,128)S(1)}, u32[]{:S(2)}, u32[]{:S(2)}) collective-permute-start(f32[12,256]{1,0:T(8,128)S(1)} %slice), channel_id=1, source_target_pairs={{0,128},{4,132},{8,136},{12,140},{16,144},{20,148},{24,152},{28,15... | collective-permute-start | bytes 36872
  271.5 17.4 %collective-permute-start.1 = (f32[16,256]{1,0:T(8,128)S(1)}, f32[16,256]{1,0:T(8,128)S(1)}, u32[]{:S(2)}, u32[]{:S(2)}) collective-permute-start(f32[16,256]{1,0:T(8,128)S(1)} %fusion), channel_id=1, source_target_pairs={{0,8},{4,12},{8,16},{12,20},{16,24},{20,28},{24,32},{28,36},{32,40... | collective-permute-start | bytes 49160
  272.8 25.0 %collective-permute-start.10 = (f32[16,256]{1,0:T(8,128)S(1)}, f32[16,256]{1,0:T(8,128)S(1)}, u32[]{:S(2)}, u32[]{:S(2)}) collective-permute-start(f32[16,256]{1,0:T(8,128)S(1)} %fusion), channel_id=1, source_target_pairs={{0,44},{4,48},{8,52},{12,56},{16,60},{20,64},{24,68},{28,72},{32,7... | collective-permute-start | bytes 49160
  274.1 25.0 %collective-permute-start.11 = (f32[16,256]{1,0:T(8,128)S(1)}, f32[16,256]{1,0:T(8,128)S(1)}, u32[]{:S(2)}, u32[]{:S(2)}) collective-permute-start(f32[16,256]{1,0:T(8,128)S(1)} %fusion), channel_id=1, source_target_pairs={{0,48},{4,52},{8,56},{12,60},{16,64},{20,68},{24,72},{28,76},{32,8... | collective-permute-start | bytes 49160
  276.5 29.1 %collective-permute-start.12 = (f32[16,256]{1,0:T(8,128)S(1)}, f32[16,256]{1,0:T(8,128)S(1)}, u32[]{:S(2)}, u32[]{:S(2)}) collective-permute-start(f32[16,256]{1,0:T(8,128)S(1)} %fusion), channel_id=1, source_target_pairs={{0,52},{4,56},{8,60},{12,64},{16,68},{20,72},{24,76},{28,80},{32,8... | collective-permute-start | bytes 49160
  283.6 24.8 %collective-permute-start.13 = (f32[16,256]{1,0:T(8,128)S(1)}, f32[16,256]{1,0:T(8,128)S(1)}, u32[]{:S(2)}, u32[]{:S(2)}) collective-permute-start(f32[16,256]{1,0:T(8,128)S(1)} %fusion), channel_id=1, source_target_pairs={{0,56},{4,60},{8,64},{12,68},{16,72},{20,76},{24,80},{28,84},{32,8... | collective-permute-start | bytes 49160
  288.9 23.5 %collective-permute-start.14 = (f32[16,256]{1,0:T(8,128)S(1)}, f32[16,256]{1,0:T(8,128)S(1)}, u32[]{:S(2)}, u32[]{:S(2)}) collective-permute-start(f32[16,256]{1,0:T(8,128)S(1)} %fusion), channel_id=1, source_target_pairs={{0,60},{4,64},{8,68},{12,72},{16,76},{20,80},{24,84},{28,88},{32,9... | collective-permute-start | bytes 49160
  297.8 17.5 %collective-permute-start.15 = (f32[16,256]{1,0:T(8,128)S(1)}, f32[16,256]{1,0:T(8,128)S(1)}, u32[]{:S(2)}, u32[]{:S(2)}) collective-permute-start(f32[16,256]{1,0:T(8,128)S(1)} %fusion), channel_id=1, source_target_pairs={{0,64},{4,68},{8,72},{12,76},{16,80},{20,84},{24,88},{28,92},{32,9... | collective-permute-start | bytes 49160
  299.1 19.2 %collective-permute-start.16 = (f32[16,256]{1,0:T(8,128)S(1)}, f32[16,256]{1,0:T(8,128)S(1)}, u32[]{:S(2)}, u32[]{:S(2)}) collective-permute-start(f32[16,256]{1,0:T(8,128)S(1)} %fusion), channel_id=1, source_target_pairs={{0,68},{4,72},{8,76},{12,80},{16,84},{20,88},{24,92},{28,96},{32,1... | collective-permute-start | bytes 49160
  305.6 14.1 %collective-permute-start.17 = (f32[16,256]{1,0:T(8,128)S(1)}, f32[16,256]{1,0:T(8,128)S(1)}, u32[]{:S(2)}, u32[]{:S(2)}) collective-permute-start(f32[16,256]{1,0:T(8,128)S(1)} %fusion), channel_id=1, source_target_pairs={{0,72},{4,76},{8,80},{12,84},{16,88},{20,92},{24,96},{28,100},{32,... | collective-permute-start | bytes 49160
  308.4 14.0 %collective-permute-start.18 = (f32[16,256]{1,0:T(8,128)S(1)}, f32[16,256]{1,0:T(8,128)S(1)}, u32[]{:S(2)}, u32[]{:S(2)}) collective-permute-start(f32[16,256]{1,0:T(8,128)S(1)} %fusion), channel_id=1, source_target_pairs={{0,76},{4,80},{8,84},{12,88},{16,92},{20,96},{24,100},{28,104},{32... | collective-permute-start | bytes 49160
  312.4 11.3 %collective-permute-start.19 = (f32[16,256]{1,0:T(8,128)S(1)}, f32[16,256]{1,0:T(8,128)S(1)}, u32[]{:S(2)}, u32[]{:S(2)}) collective-permute-start(f32[16,256]{1,0:T(8,128)S(1)} %fusion), channel_id=1, source_target_pairs={{0,80},{4,84},{8,88},{12,92},{16,96},{20,100},{24,104},{28,108},{3... | collective-permute-start | bytes 49160
  315.3 9.8 %collective-permute-start.2 = (f32[16,256]{1,0:T(8,128)S(1)}, f32[16,256]{1,0:T(8,128)S(1)}, u32[]{:S(2)}, u32[]{:S(2)}) collective-permute-start(f32[16,256]{1,0:T(8,128)S(1)} %fusion), channel_id=1, source_target_pairs={{0,12},{4,16},{8,20},{12,24},{16,28},{20,32},{24,36},{28,40},{32,4... | collective-permute-start | bytes 49160
  318.3 8.5 %collective-permute-start.20 = (f32[16,256]{1,0:T(8,128)S(1)}, f32[16,256]{1,0:T(8,128)S(1)}, u32[]{:S(2)}, u32[]{:S(2)}) collective-permute-start(f32[16,256]{1,0:T(8,128)S(1)} %fusion), channel_id=1, source_target_pairs={{0,84},{4,88},{8,92},{12,96},{16,100},{20,104},{24,108},{28,112},{... | collective-permute-start | bytes 49160
  319.7 8.8 %collective-permute-start.21 = (f32[16,256]{1,0:T(8,128)S(1)}, f32[16,256]{1,0:T(8,128)S(1)}, u32[]{:S(2)}, u32[]{:S(2)}) collective-permute-start(f32[16,256]{1,0:T(8,128)S(1)} %fusion), channel_id=1, source_target_pairs={{0,88},{4,92},{8,96},{12,100},{16,104},{20,108},{24,112},{28,116},... | collective-permute-start | bytes 49160
  322.4 9.4 %collective-permute-start.22 = (f32[16,256]{1,0:T(8,128)S(1)}, f32[16,256]{1,0:T(8,128)S(1)}, u32[]{:S(2)}, u32[]{:S(2)}) collective-permute-start(f32[16,256]{1,0:T(8,128)S(1)} %fusion), channel_id=1, source_target_pairs={{0,92},{4,96},{8,100},{12,104},{16,108},{20,112},{24,116},{28,120}... | collective-permute-start | bytes 49160
  323.7 10.9 %collective-permute-start.23 = (f32[16,256]{1,0:T(8,128)S(1)}, f32[16,256]{1,0:T(8,128)S(1)}, u32[]{:S(2)}, u32[]{:S(2)}) collective-permute-start(f32[16,256]{1,0:T(8,128)S(1)} %fusion), channel_id=1, source_target_pairs={{0,96},{4,100},{8,104},{12,108},{16,112},{20,116},{24,120},{28,124... | collective-permute-start | bytes 49160
  325.0 11.5 %collective-permute-start.24 = (f32[16,256]{1,0:T(8,128)S(1)}, f32[16,256]{1,0:T(8,128)S(1)}, u32[]{:S(2)}, u32[]{:S(2)}) collective-permute-start(f32[16,256]{1,0:T(8,128)S(1)} %fusion), channel_id=1, source_target_pairs={{0,100},{4,104},{8,108},{12,112},{16,116},{20,120},{24,124},{28,12... | collective-permute-start | bytes 49160
  326.9 11.4 %collective-permute-start.25 = (f32[16,256]{1,0:T(8,128)S(1)}, f32[16,256]{1,0:T(8,128)S(1)}, u32[]{:S(2)}, u32[]{:S(2)}) collective-permute-start(f32[16,256]{1,0:T(8,128)S(1)} %fusion), channel_id=1, source_target_pairs={{0,104},{4,108},{8,112},{12,116},{16,120},{20,124},{24,128},{28,13... | collective-permute-start | bytes 49160
  328.5 12.3 %collective-permute-start.26 = (f32[16,256]{1,0:T(8,128)S(1)}, f32[16,256]{1,0:T(8,128)S(1)}, u32[]{:S(2)}, u32[]{:S(2)}) collective-permute-start(f32[16,256]{1,0:T(8,128)S(1)} %fusion), channel_id=1, source_target_pairs={{0,108},{4,112},{8,116},{12,120},{16,124},{20,128},{24,132},{28,13... | collective-permute-start | bytes 49160
  331.8 10.9 %collective-permute-start.27 = (f32[16,256]{1,0:T(8,128)S(1)}, f32[16,256]{1,0:T(8,128)S(1)}, u32[]{:S(2)}, u32[]{:S(2)}) collective-permute-start(f32[16,256]{1,0:T(8,128)S(1)} %fusion), channel_id=1, source_target_pairs={{0,112},{4,116},{8,120},{12,124},{16,128},{20,132},{24,136},{28,14... | collective-permute-start | bytes 49160
  334.7 12.6 %collective-permute-start.28 = (f32[16,256]{1,0:T(8,128)S(1)}, f32[16,256]{1,0:T(8,128)S(1)}, u32[]{:S(2)}, u32[]{:S(2)}) collective-permute-start(f32[16,256]{1,0:T(8,128)S(1)} %fusion), channel_id=1, source_target_pairs={{0,116},{4,120},{8,124},{12,128},{16,132},{20,136},{24,140},{28,14... | collective-permute-start | bytes 49160
  336.6 11.9 %collective-permute-start.29 = (f32[16,256]{1,0:T(8,128)S(1)}, f32[16,256]{1,0:T(8,128)S(1)}, u32[]{:S(2)}, u32[]{:S(2)}) collective-permute-start(f32[16,256]{1,0:T(8,128)S(1)} %fusion), channel_id=1, source_target_pairs={{0,120},{4,124},{8,128},{12,132},{16,136},{20,140},{24,144},{28,14... | collective-permute-start | bytes 49160
  338.2 12.5 %collective-permute-start.3 = (f32[16,256]{1,0:T(8,128)S(1)}, f32[16,256]{1,0:T(8,128)S(1)}, u32[]{:S(2)}, u32[]{:S(2)}) collective-permute-start(f32[16,256]{1,0:T(8,128)S(1)} %fusion), channel_id=1, source_target_pairs={{0,16},{4,20},{8,24},{12,28},{16,32},{20,36},{24,40},{28,44},{32,4... | collective-permute-start | bytes 49160
  340.9 12.9 %collective-permute-start.30 = (f32[16,256]{1,0:T(8,128)S(1)}, f32[16,256]{1,0:T(8,128)S(1)}, u32[]{:S(2)}, u32[]{:S(2)}) collective-permute-start(f32[16,256]{1,0:T(8,128)S(1)} %fusion), channel_id=1, source_target_pairs={{0,124},{4,128},{8,132},{12,136},{16,140},{20,144},{24,148},{28,15... | collective-permute-start | bytes 49160
  342.7 14.7 %collective-permute-start.4 = (f32[16,256]{1,0:T(8,128)S(1)}, f32[16,256]{1,0:T(8,128)S(1)}, u32[]{:S(2)}, u32[]{:S(2)}) collective-permute-start(f32[16,256]{1,0:T(8,128)S(1)} %fusion), channel_id=1, source_target_pairs={{0,20},{4,24},{8,28},{12,32},{16,36},{20,40},{24,44},{28,48},{32,5... | collective-permute-start | bytes 49160
  347.2 13.5 %collective-permute-start.5 = (f32[16,256]{1,0:T(8,128)S(1)}, f32[16,256]{1,0:T(8,128)S(1)}, u32[]{:S(2)}, u32[]{:S(2)}) collective-permute-start(f32[16,256]{1,0:T(8,128)S(1)} %fusion), channel_id=1, source_target_pairs={{0,24},{4,28},{8,32},{12,36},{16,40},{20,44},{24,48},{28,52},{32,5... | collective-permute-start | bytes 49160
  348.5 12.2 %collective-permute-start.6 = (f32[16,256]{1,0:T(8,128)S(1)}, f32[16,256]{1,0:T(8,128)S(1)}, u32[]{:S(2)}, u32[]{:S(2)}) collective-permute-start(f32[16,256]{1,0:T(8,128)S(1)} %fusion), channel_id=1, source_target_pairs={{0,28},{4,32},{8,36},{12,40},{16,44},{20,48},{24,52},{28,56},{32,6... | collective-permute-start | bytes 49160
  350.8 9.9 %collective-permute-start.7 = (f32[16,256]{1,0:T(8,128)S(1)}, f32[16,256]{1,0:T(8,128)S(1)}, u32[]{:S(2)}, u32[]{:S(2)}) collective-permute-start(f32[16,256]{1,0:T(8,128)S(1)} %fusion), channel_id=1, source_target_pairs={{0,32},{4,36},{8,40},{12,44},{16,48},{20,52},{24,56},{28,60},{32,6... | collective-permute-start | bytes 49160
  353.8 6.9 %collective-permute-start.8 = (f32[16,256]{1,0:T(8,128)S(1)}, f32[16,256]{1,0:T(8,128)S(1)}, u32[]{:S(2)}, u32[]{:S(2)}) collective-permute-start(f32[16,256]{1,0:T(8,128)S(1)} %fusion), channel_id=1, source_target_pairs={{0,36},{4,40},{8,44},{12,48},{16,52},{20,56},{24,60},{28,64},{32,6... | collective-permute-start | bytes 49160
  357.5 3.3 collective-permute-start.9
  468.7 101.6 %copy-start = (f32[12,256]{1,0:T(8,128)}, f32[12,256]{1,0:T(8,128)S(1)}, u32[]{:S(2)}) copy-start(f32[12,256]{1,0:T(8,128)S(1)} %get-tuple-element.6) | copy-start | bytes 36868
where the time goes:
time: 572 us; the launch traced here: 570 us
  blocking collectives  465 us (81%)
  starting transfers between devices  92.4 us (16%)
  local copies, waits for them, and re-layouts  6.01 us (1%)
    unnamed x1, blocking collectives  263 us
    psum x1, blocking collectives, shards(): sq = lax.psum(jnp.sum(grad_part * grad_part), ('shard', 'tensor'))  102 us
    all_gather x1, blocking collectives, shards(): lax.all_gather(new_master.astype(jnp.bfloat16), 'shard', axis=0, tiled=True)  100 us
    unnamed x32, starting transfers between devices  92.4 us
  transfers between devices with their start and end apart: 32, of which 0 were waited for; matrix products, arithmetic and copies ran while one was open for 0% of the time, Pallas kernels for 0%

commit v1 on v0

--- a/solution.py
+++ b/solution.py
@@ -27,7 +27,11 @@
         first_hat / (jnp.sqrt(second_hat) + 1e-08) + decay_weight * master
     )
     new_ema = ema_keep * ema + (1.0 - ema_keep) * new_master
-    weights = lax.all_gather(new_master.astype(jnp.bfloat16), "shard", axis=0, tiled=True)
+    t0 = new_master.astype(jnp.bfloat16)
+    heard = tuple((t0 for _ in range(lax.axis_size("shard"))))
+    z = jnp.stack(heard, axis=0)
+    front = lax.all_to_all(z, "shard", 0, 0)
+    weights = jnp.concatenate(front, axis=0)
     return (new_master, new_moment1, new_moment2, new_ema, weights)
 
 

time: 572 us -> 537 us (0.939)
  blocking collectives: 465 us -> 365 us
  waiting for transfers between devices: 0.08 us -> 51.3 us
  starting transfers between devices: 92.4 us -> 102 us
    all_gather x1 -> x0, blocking collectives: 100 us -> none  [shards(): lax.all_gather(new_master.astype(jnp.bfloat16), 'shard', axis=0, tiled=True)]
    all_to_all x0 -> x1, waiting for transfers between devices: none -> 51.2 us  [shards(): front = lax.all_to_all(z, 'shard', 0, 0)]
    all_to_all x0 -> x1, starting transfers between devices: none -> 9.92 us  [shards(): front = lax.all_to_all(z, 'shard', 0, 0)]
  transfers between devices with their start and end apart: 32 -> 33, of which waited for: 0 -> 1; matrix products, arithmetic and copies ran while one was open for 0% -> 0% of each run, Pallas kernels for 0% -> 0%
where the time goes in v1:
time: 537 us; the launch traced here: 533 us
  blocking collectives  365 us (68%)
  starting transfers between devices  102 us (19%)
  waiting for transfers between devices  51.3 us (10%)
  local copies, waits for them, and re-layouts  7.09 us (1%)
    unnamed x1, blocking collectives  263 us
    psum x1, blocking collectives, shards(): sq = lax.psum(jnp.sum(grad_part * grad_part), ('shard', 'tensor'))  102 us
    unnamed x32, starting transfers between devices  92.4 us
    all_to_all x1, waiting for transfers between devices, shards(): front = lax.all_to_all(z, 'shard', 0, 0)  51.2 us
  transfers between devices with their start and end apart: 33, of which 1 were waited for; matrix products, arithmetic and copies ran while one was open for 0% of the time, Pallas kernels for 0%

profile of v1, /device:TPU:1, one launch (start us, length us, event | category | flops | bytes accessed | tf_op | source)
XLA Modules:
  0.0 532.6 jit_solution(195749372045197919)
XLA Ops:
  0.6 2.5 convert_reduce_fusion
  3.1 0.0 copy-start.2
  3.1 0.0 copy-start.3
  3.1 0.0 copy-start.4
  3.2 262.6 %fusion = f32[16,256]{1,0:T(8,128)S(1)} fusion(f32[1536,256]{1,0:T(8,128)S(1)} %convert_reduce_fusion), kind=kCustom, calls=%all-reduce-scatter | all-reduce-scatter fusion | flops 524289 | bytes 1591296
  265.8 3.0 collective-permute-start
  268.8 2.6 collective-permute-start.31
  271.5 1.3 collective-permute-start.1
  272.8 1.3 collective-permute-start.10
  274.1 2.4 collective-permute-start.11
  276.5 7.0 %collective-permute-start.12 = (f32[16,256]{1,0:T(8,128)S(1)}, f32[16,256]{1,0:T(8,128)S(1)}, u32[]{:S(2)}, u32[]{:S(2)}) collective-permute-start(f32[16,256]{1,0:T(8,128)S(1)} %fusion), channel_id=1, source_target_pairs={{0,52},{4,56},{8,60},{12,64},{16,68},{20,72},{24,76},{28,80},{32,8... | collective-permute-start | bytes 49160
  283.6 5.3 collective-permute-start.13
  288.9 8.9 %collective-permute-start.14 = (f32[16,256]{1,0:T(8,128)S(1)}, f32[16,256]{1,0:T(8,128)S(1)}, u32[]{:S(2)}, u32[]{:S(2)}) collective-permute-start(f32[16,256]{1,0:T(8,128)S(1)} %fusion), channel_id=1, source_target_pairs={{0,60},{4,64},{8,68},{12,72},{16,76},{20,80},{24,84},{28,88},{32,9... | collective-permute-start | bytes 49160
  297.8 1.3 collective-permute-start.15
  299.1 6.5 %collective-permute-start.16 = (f32[16,256]{1,0:T(8,128)S(1)}, f32[16,256]{1,0:T(8,128)S(1)}, u32[]{:S(2)}, u32[]{:S(2)}) collective-permute-start(f32[16,256]{1,0:T(8,128)S(1)} %fusion), channel_id=1, source_target_pairs={{0,68},{4,72},{8,76},{12,80},{16,84},{20,88},{24,92},{28,96},{32,1... | collective-permute-start | bytes 49160
  305.6 2.8 collective-permute-start.17
  308.4 4.0 collective-permute-start.18
  312.4 2.9 collective-permute-start.19
  315.3 3.0 collective-permute-start.2
  318.3 1.4 collective-permute-start.20
  319.7 2.7 collective-permute-start.21
  322.4 1.3 collective-permute-start.22
  323.7 1.3 collective-permute-start.23
  325.0 1.8 collective-permute-start.24
  326.9 1.6 collective-permute-start.25
  328.5 3.2 collective-permute-start.26
  331.8 2.8 collective-permute-start.27
  334.7 1.9 collective-permute-start.28
  336.6 1.6 collective-permute-start.29
  338.2 2.6 collective-permute-start.3
  340.9 1.8 collective-permute-start.30
  342.7 4.5 collective-permute-start.4
  347.2 1.3 collective-permute-start.5
  348.5 2.2 collective-permute-start.6
  350.8 3.0 collective-permute-start.7
  353.8 3.7 collective-permute-start.8
  357.4 1.3 collective-permute-start.9
  358.7 1.3 dynamic-slice.4
  360.7 0.0 copy-start.1
  360.7 3.7 concatenate
  364.4 0.6 multiply_reduce_fusion
  365.0 102.4 %psum.7 = f32[]{:T(128)} all-reduce(f32[]{:T(128)} %multiply_reduce_fusion), channel_id=1, replica_groups=mesh['shard'=128,'tensor'=4] {'shard','tensor'}, use_global_device_ids=true, to_apply=%region_3.0 | all-reduce | flops 1 | bytes 8 | tf_op jit(solution)/shard_map/psum | solution.py:19
  468.1 0.6 fusion.2
  468.7 1.1 stack.2
  469.8 9.9 %all-to-all-start = ((bf16[128,12,256]{2,1,0:T(8,128)(2,1)}), bf16[128,12,256]{2,1,0:T(8,128)(2,1)S(1)}, u32[]{:S(2)}, u32[]{:S(2)}) async-start(bf16[128,12,256]{2,1,0:T(8,128)(2,1)} %stack.2), calls=%async_computation | async-start | bytes 2097152 | tf_op jit(solution)/shard_map/all_to_all | solution.py:33
  479.7 0.6 multiply_add_fusion
  480.4 51.2 %all-to-all-done = bf16[128,12,256]{2,1,0:T(8,128)(2,1)S(1)} async-done(((bf16[128,12,256]{2,1,0:T(8,128)(2,1)}), bf16[128,12,256]{2,1,0:T(8,128)(2,1)S(1)}, u32[]{:S(2)}, u32[]{:S(2)}) %all-to-all-start) | async-done | bytes 786464 | tf_op jit(solution)/shard_map/all_to_all | solution.py:33
  531.6 1.1 reshape.16
  (39 shorter events, 0.1 us)
Async XLA Ops:
  3.1 465.0 %copy-start.2 = (f32[12,256]{1,0:T(8,128)S(1)}, f32[12,256]{1,0:T(8,128)}, u32[]{:S(2)}) copy-start(f32[12,256]{1,0:T(8,128)} %param.6) | copy-start | bytes 36868
  3.1 464.9 %copy-start.3 = (f32[12,256]{1,0:T(8,128)S(1)}, f32[12,256]{1,0:T(8,128)}, u32[]{:S(2)}) copy-start(f32[12,256]{1,0:T(8,128)} %param.7) | copy-start | bytes 36868
  3.1 464.9 %copy-start.4 = (f32[12,256]{1,0:T(8,128)S(1)}, f32[12,256]{1,0:T(8,128)}, u32[]{:S(2)}) copy-start(f32[12,256]{1,0:T(8,128)} %param.8) | copy-start | bytes 36868
  265.8 17.7 %collective-permute-start = (f32[16,256]{1,0:T(8,128)S(1)}, f32[16,256]{1,0:T(8,128)S(1)}, u32[]{:S(2)}, u32[]{:S(2)}) collective-permute-start(f32[16,256]{1,0:T(8,128)S(1)} %fusion), channel_id=1, source_target_pairs={{0,4},{4,8},{8,12},{12,16},{16,20},{20,24},{24,28},{28,32},{32,36}... | collective-permute-start | bytes 49160
  268.8 7.7 %collective-permute-start.31 = (f32[12,256]{1,0:T(8,128)S(1)}, f32[12,256]{1,0:T(8,128)S(1)}, u32[]{:S(2)}, u32[]{:S(2)}) collective-permute-start(f32[12,256]{1,0:T(8,128)S(1)} %slice), channel_id=1, source_target_pairs={{0,128},{4,132},{8,136},{12,140},{16,144},{20,148},{24,152},{28,15... | collective-permute-start | bytes 36872
  271.5 17.4 %collective-permute-start.1 = (f32[16,256]{1,0:T(8,128)S(1)}, f32[16,256]{1,0:T(8,128)S(1)}, u32[]{:S(2)}, u32[]{:S(2)}) collective-permute-start(f32[16,256]{1,0:T(8,128)S(1)} %fusion), channel_id=1, source_target_pairs={{0,8},{4,12},{8,16},{12,20},{16,24},{20,28},{24,32},{28,36},{32,40... | collective-permute-start | bytes 49160
  272.8 25.0 %collective-permute-start.10 = (f32[16,256]{1,0:T(8,128)S(1)}, f32[16,256]{1,0:T(8,128)S(1)}, u32[]{:S(2)}, u32[]{:S(2)}) collective-permute-start(f32[16,256]{1,0:T(8,128)S(1)} %fusion), channel_id=1, source_target_pairs={{0,44},{4,48},{8,52},{12,56},{16,60},{20,64},{24,68},{28,72},{32,7... | collective-permute-start | bytes 49160
  274.1 25.0 %collective-permute-start.11 = (f32[16,256]{1,0:T(8,128)S(1)}, f32[16,256]{1,0:T(8,128)S(1)}, u32[]{:S(2)}, u32[]{:S(2)}) collective-permute-start(f32[16,256]{1,0:T(8,128)S(1)} %fusion), channel_id=1, source_target_pairs={{0,48},{4,52},{8,56},{12,60},{16,64},{20,68},{24,72},{28,76},{32,8... | collective-permute-start | bytes 49160
  276.5 29.1 %collective-permute-start.12 = (f32[16,256]{1,0:T(8,128)S(1)}, f32[16,256]{1,0:T(8,128)S(1)}, u32[]{:S(2)}, u32[]{:S(2)}) collective-permute-start(f32[16,256]{1,0:T(8,128)S(1)} %fusion), channel_id=1, source_target_pairs={{0,52},{4,56},{8,60},{12,64},{16,68},{20,72},{24,76},{28,80},{32,8... | collective-permute-start | bytes 49160
  283.6 24.8 %collective-permute-start.13 = (f32[16,256]{1,0:T(8,128)S(1)}, f32[16,256]{1,0:T(8,128)S(1)}, u32[]{:S(2)}, u32[]{:S(2)}) collective-permute-start(f32[16,256]{1,0:T(8,128)S(1)} %fusion), channel_id=1, source_target_pairs={{0,56},{4,60},{8,64},{12,68},{16,72},{20,76},{24,80},{28,84},{32,8... | collective-permute-start | bytes 49160
  288.9 23.5 %collective-permute-start.14 = (f32[16,256]{1,0:T(8,128)S(1)}, f32[16,256]{1,0:T(8,128)S(1)}, u32[]{:S(2)}, u32[]{:S(2)}) collective-permute-start(f32[16,256]{1,0:T(8,128)S(1)} %fusion), channel_id=1, source_target_pairs={{0,60},{4,64},{8,68},{12,72},{16,76},{20,80},{24,84},{28,88},{32,9... | collective-permute-start | bytes 49160
  297.8 17.5 %collective-permute-start.15 = (f32[16,256]{1,0:T(8,128)S(1)}, f32[16,256]{1,0:T(8,128)S(1)}, u32[]{:S(2)}, u32[]{:S(2)}) collective-permute-start(f32[16,256]{1,0:T(8,128)S(1)} %fusion), channel_id=1, source_target_pairs={{0,64},{4,68},{8,72},{12,76},{16,80},{20,84},{24,88},{28,92},{32,9... | collective-permute-start | bytes 49160
  299.1 19.2 %collective-permute-start.16 = (f32[16,256]{1,0:T(8,128)S(1)}, f32[16,256]{1,0:T(8,128)S(1)}, u32[]{:S(2)}, u32[]{:S(2)}) collective-permute-start(f32[16,256]{1,0:T(8,128)S(1)} %fusion), channel_id=1, source_target_pairs={{0,68},{4,72},{8,76},{12,80},{16,84},{20,88},{24,92},{28,96},{32,1... | collective-permute-start | bytes 49160
  305.6 14.1 %collective-permute-start.17 = (f32[16,256]{1,0:T(8,128)S(1)}, f32[16,256]{1,0:T(8,128)S(1)}, u32[]{:S(2)}, u32[]{:S(2)}) collective-permute-start(f32[16,256]{1,0:T(8,128)S(1)} %fusion), channel_id=1, source_target_pairs={{0,72},{4,76},{8,80},{12,84},{16,88},{20,92},{24,96},{28,100},{32,... | collective-permute-start | bytes 49160
  308.4 14.0 %collective-permute-start.18 = (f32[16,256]{1,0:T(8,128)S(1)}, f32[16,256]{1,0:T(8,128)S(1)}, u32[]{:S(2)}, u32[]{:S(2)}) collective-permute-start(f32[16,256]{1,0:T(8,128)S(1)} %fusion), channel_id=1, source_target_pairs={{0,76},{4,80},{8,84},{12,88},{16,92},{20,96},{24,100},{28,104},{32... | collective-permute-start | bytes 49160
  312.4 11.3 %collective-permute-start.19 = (f32[16,256]{1,0:T(8,128)S(1)}, f32[16,256]{1,0:T(8,128)S(1)}, u32[]{:S(2)}, u32[]{:S(2)}) collective-permute-start(f32[16,256]{1,0:T(8,128)S(1)} %fusion), channel_id=1, source_target_pairs={{0,80},{4,84},{8,88},{12,92},{16,96},{20,100},{24,104},{28,108},{3... | collective-permute-start | bytes 49160
  315.3 9.8 %collective-permute-start.2 = (f32[16,256]{1,0:T(8,128)S(1)}, f32[16,256]{1,0:T(8,128)S(1)}, u32[]{:S(2)}, u32[]{:S(2)}) collective-permute-start(f32[16,256]{1,0:T(8,128)S(1)} %fusion), channel_id=1, source_target_pairs={{0,12},{4,16},{8,20},{12,24},{16,28},{20,32},{24,36},{28,40},{32,4... | collective-permute-start | bytes 49160
  318.3 8.5 %collective-permute-start.20 = (f32[16,256]{1,0:T(8,128)S(1)}, f32[16,256]{1,0:T(8,128)S(1)}, u32[]{:S(2)}, u32[]{:S(2)}) collective-permute-start(f32[16,256]{1,0:T(8,128)S(1)} %fusion), channel_id=1, source_target_pairs={{0,84},{4,88},{8,92},{12,96},{16,100},{20,104},{24,108},{28,112},{... | collective-permute-start | bytes 49160
  319.7 8.8 %collective-permute-start.21 = (f32[16,256]{1,0:T(8,128)S(1)}, f32[16,256]{1,0:T(8,128)S(1)}, u32[]{:S(2)}, u32[]{:S(2)}) collective-permute-start(f32[16,256]{1,0:T(8,128)S(1)} %fusion), channel_id=1, source_target_pairs={{0,88},{4,92},{8,96},{12,100},{16,104},{20,108},{24,112},{28,116},... | collective-permute-start | bytes 49160
  322.4 9.4 %collective-permute-start.22 = (f32[16,256]{1,0:T(8,128)S(1)}, f32[16,256]{1,0:T(8,128)S(1)}, u32[]{:S(2)}, u32[]{:S(2)}) collective-permute-start(f32[16,256]{1,0:T(8,128)S(1)} %fusion), channel_id=1, source_target_pairs={{0,92},{4,96},{8,100},{12,104},{16,108},{20,112},{24,116},{28,120}... | collective-permute-start | bytes 49160
  323.7 10.9 %collective-permute-start.23 = (f32[16,256]{1,0:T(8,128)S(1)}, f32[16,256]{1,0:T(8,128)S(1)}, u32[]{:S(2)}, u32[]{:S(2)}) collective-permute-start(f32[16,256]{1,0:T(8,128)S(1)} %fusion), channel_id=1, source_target_pairs={{0,96},{4,100},{8,104},{12,108},{16,112},{20,116},{24,120},{28,124... | collective-permute-start | bytes 49160
  325.0 11.5 %collective-permute-start.24 = (f32[16,256]{1,0:T(8,128)S(1)}, f32[16,256]{1,0:T(8,128)S(1)}, u32[]{:S(2)}, u32[]{:S(2)}) collective-permute-start(f32[16,256]{1,0:T(8,128)S(1)} %fusion), channel_id=1, source_target_pairs={{0,100},{4,104},{8,108},{12,112},{16,116},{20,120},{24,124},{28,12... | collective-permute-start | bytes 49160
  326.9 11.4 %collective-permute-start.25 = (f32[16,256]{1,0:T(8,128)S(1)}, f32[16,256]{1,0:T(8,128)S(1)}, u32[]{:S(2)}, u32[]{:S(2)}) collective-permute-start(f32[16,256]{1,0:T(8,128)S(1)} %fusion), channel_id=1, source_target_pairs={{0,104},{4,108},{8,112},{12,116},{16,120},{20,124},{24,128},{28,13... | collective-permute-start | bytes 49160
  328.5 12.3 %collective-permute-start.26 = (f32[16,256]{1,0:T(8,128)S(1)}, f32[16,256]{1,0:T(8,128)S(1)}, u32[]{:S(2)}, u32[]{:S(2)}) collective-permute-start(f32[16,256]{1,0:T(8,128)S(1)} %fusion), channel_id=1, source_target_pairs={{0,108},{4,112},{8,116},{12,120},{16,124},{20,128},{24,132},{28,13... | collective-permute-start | bytes 49160
  331.8 10.9 %collective-permute-start.27 = (f32[16,256]{1,0:T(8,128)S(1)}, f32[16,256]{1,0:T(8,128)S(1)}, u32[]{:S(2)}, u32[]{:S(2)}) collective-permute-start(f32[16,256]{1,0:T(8,128)S(1)} %fusion), channel_id=1, source_target_pairs={{0,112},{4,116},{8,120},{12,124},{16,128},{20,132},{24,136},{28,14... | collective-permute-start | bytes 49160
  334.7 12.6 %collective-permute-start.28 = (f32[16,256]{1,0:T(8,128)S(1)}, f32[16,256]{1,0:T(8,128)S(1)}, u32[]{:S(2)}, u32[]{:S(2)}) collective-permute-start(f32[16,256]{1,0:T(8,128)S(1)} %fusion), channel_id=1, source_target_pairs={{0,116},{4,120},{8,124},{12,128},{16,132},{20,136},{24,140},{28,14... | collective-permute-start | bytes 49160
  336.6 11.9 %collective-permute-start.29 = (f32[16,256]{1,0:T(8,128)S(1)}, f32[16,256]{1,0:T(8,128)S(1)}, u32[]{:S(2)}, u32[]{:S(2)}) collective-permute-start(f32[16,256]{1,0:T(8,128)S(1)} %fusion), channel_id=1, source_target_pairs={{0,120},{4,124},{8,128},{12,132},{16,136},{20,140},{24,144},{28,14... | collective-permute-start | bytes 49160
  338.2 12.5 %collective-permute-start.3 = (f32[16,256]{1,0:T(8,128)S(1)}, f32[16,256]{1,0:T(8,128)S(1)}, u32[]{:S(2)}, u32[]{:S(2)}) collective-permute-start(f32[16,256]{1,0:T(8,128)S(1)} %fusion), channel_id=1, source_target_pairs={{0,16},{4,20},{8,24},{12,28},{16,32},{20,36},{24,40},{28,44},{32,4... | collective-permute-start | bytes 49160
  340.9 12.9 %collective-permute-start.30 = (f32[16,256]{1,0:T(8,128)S(1)}, f32[16,256]{1,0:T(8,128)S(1)}, u32[]{:S(2)}, u32[]{:S(2)}) collective-permute-start(f32[16,256]{1,0:T(8,128)S(1)} %fusion), channel_id=1, source_target_pairs={{0,124},{4,128},{8,132},{12,136},{16,140},{20,144},{24,148},{28,15... | collective-permute-start | bytes 49160
  342.7 14.7 %collective-permute-start.4 = (f32[16,256]{1,0:T(8,128)S(1)}, f32[16,256]{1,0:T(8,128)S(1)}, u32[]{:S(2)}, u32[]{:S(2)}) collective-permute-start(f32[16,256]{1,0:T(8,128)S(1)} %fusion), channel_id=1, source_target_pairs={{0,20},{4,24},{8,28},{12,32},{16,36},{20,40},{24,44},{28,48},{32,5... | collective-permute-start | bytes 49160
  347.2 13.5 %collective-permute-start.5 = (f32[16,256]{1,0:T(8,128)S(1)}, f32[16,256]{1,0:T(8,128)S(1)}, u32[]{:S(2)}, u32[]{:S(2)}) collective-permute-start(f32[16,256]{1,0:T(8,128)S(1)} %fusion), channel_id=1, source_target_pairs={{0,24},{4,28},{8,32},{12,36},{16,40},{20,44},{24,48},{28,52},{32,5... | collective-permute-start | bytes 49160
  348.5 12.2 %collective-permute-start.6 = (f32[16,256]{1,0:T(8,128)S(1)}, f32[16,256]{1,0:T(8,128)S(1)}, u32[]{:S(2)}, u32[]{:S(2)}) collective-permute-start(f32[16,256]{1,0:T(8,128)S(1)} %fusion), channel_id=1, source_target_pairs={{0,28},{4,32},{8,36},{12,40},{16,44},{20,48},{24,52},{28,56},{32,6... | collective-permute-start | bytes 49160
  350.8 9.9 %collective-permute-start.7 = (f32[16,256]{1,0:T(8,128)S(1)}, f32[16,256]{1,0:T(8,128)S(1)}, u32[]{:S(2)}, u32[]{:S(2)}) collective-permute-start(f32[16,256]{1,0:T(8,128)S(1)} %fusion), channel_id=1, source_target_pairs={{0,32},{4,36},{8,40},{12,44},{16,48},{20,52},{24,56},{28,60},{32,6... | collective-permute-start | bytes 49160
  353.8 6.9 %collective-permute-start.8 = (f32[16,256]{1,0:T(8,128)S(1)}, f32[16,256]{1,0:T(8,128)S(1)}, u32[]{:S(2)}, u32[]{:S(2)}) collective-permute-start(f32[16,256]{1,0:T(8,128)S(1)} %fusion), channel_id=1, source_target_pairs={{0,36},{4,40},{8,44},{12,48},{16,52},{20,56},{24,60},{28,64},{32,6... | collective-permute-start | bytes 49160
  357.4 3.3 collective-permute-start.9
  360.7 119.1 %copy-start.1 = (f32[12,256]{1,0:T(8,128)S(1)}, f32[12,256]{1,0:T(8,128)}, u32[]{:S(2)}) copy-start(f32[12,256]{1,0:T(8,128)} %param.9) | copy-start | bytes 36868
  468.7 63.9 %copy-start = (f32[12,256]{1,0:T(8,128)}, f32[12,256]{1,0:T(8,128)S(1)}, u32[]{:S(2)}) copy-start(f32[12,256]{1,0:T(8,128)S(1)} %get-tuple-element.6) | copy-start | bytes 36868
  469.8 61.8 %all-to-all-start = ((bf16[128,12,256]{2,1,0:T(8,128)(2,1)}), bf16[128,12,256]{2,1,0:T(8,128)(2,1)S(1)}, u32[]{:S(2)}, u32[]{:S(2)}) async-start(bf16[128,12,256]{2,1,0:T(8,128)(2,1)} %stack.2), calls=%async_computation | async-start | bytes 2097152 | tf_op jit(solution)/shard_map/all_to_all | solution.py:33
